TPU v7x, 32 devices: a whole 2x2x4 slice. The times are simulated.
32 devices in a mesh: rep: 2 (over x), zero: 16 (over z, y, core).
Axes of the slice: x: 2, y: 2, z: 4, core: 2. Of those that a mesh axis runs over, the one named last changes fastest.
Arguments:
- gated_input: bfloat16 [2, 2048, 4096], P('rep', 'zero'), may hold values from -6 to 6
- query_gate: bfloat16 [2, 2048, 4096], P('rep', 'zero'), may hold values from -12 to 12
- cotangent: bfloat16 [2, 2048, 4096], P('rep', 'zero'), may hold values from -8 to 8
- filters: float32 [2, 256, 128], P('rep', 'zero'), may hold values from -0.5 to 0.5
- first_moment: float32 [2, 256, 128], P('rep', 'zero'), may hold values from -0.03125 to 0.03125
- second_moment: float32 [2, 256, 128], P('rep', 'zero'), may hold values from 1e-06 to 0.0001
- step_index: int32 [1], replicated, may hold values from 0 to 999
Outputs:
- query_grad: bfloat16 [2, 2048, 4096], P('rep', 'zero')
- input_grad: bfloat16 [2, 2048, 4096], P('rep', 'zero')
- new_filters: float32 [2, 256, 128], P('rep', 'zero')
All inputs are finite; a program needn't handle non-finite values.
Results may differ from a plain program's by a relative error of at most 0.007.
Values may be sent and summed in bfloat16 or wider, within the bound.
No kernel may reach another device: no remote copies, remote signals or barrier semaphores. Data moves between devices by JAX's collectives and lax.ppermute only.
A program may use at most 256 MiB of HBM per device.

v0:
```python
from functools import partial
import jax
import jax.numpy as jnp
from jax import lax
from jax.sharding import PartitionSpec as P

CLIP_NORM = 1.0
BETA_ONE = 0.9
BETA_TWO = 0.95
LEARN_RATE = 0.05
ADAM_EPS = 1e-08


def swapped(value, axis, apart):
    mask = 2**apart
    pairs = [(source, source ^ mask) for source in range(lax.axis_size(axis))]
    return lax.ppermute(value, axis, pairs)


def passed_along(block, axis, distance):
    devices = range(lax.axis_size(axis))
    route = [(i - distance, i) for i in devices if i - distance in devices]
    return lax.ppermute(block, axis, route)


def circulant(half_filters):
    groups_all, filter_len = half_filters.shape
    flipped = half_filters[:, ::-1]
    doubled = jnp.concatenate([flipped, flipped], axis=1)
    tiled = jnp.tile(doubled, (1, filter_len))
    trimmed = tiled[:, : filter_len * (2 * filter_len - 1)]
    return trimmed.reshape(groups_all, filter_len, 2 * filter_len - 1)[:, :, filter_len - 1 :]


def blocked(rows_major, groups_all, filter_len):
    tok_rows, channels = rows_major.shape
    return rows_major.T.reshape(
        groups_all, channels // groups_all, tok_rows // filter_len, filter_len
    )


def unblocked(blocks):
    groups_all, group_width, block_count, filter_len = blocks.shape
    return blocks.reshape(groups_all * group_width, block_count * filter_len).T


def swap_bit(values, bit_number):
    return swapped(values, "rep", bit_number)


def on_device(gated_input, query_gate, cotangent, filters, first_moment, second_moment, step_index):
    inputs = gated_input[0]
    gate_values = query_gate[0]
    upstream = cotangent[0]
    tok_rows, channels = inputs.shape
    filter_len = filters.shape[2]
    shard_len = filters.shape[1]
    half_filters = lax.all_gather(filters[0].astype(jnp.bfloat16), "zero", axis=0, tiled=True)
    groups_all = half_filters.shape[0]
    circ_table = circulant(half_filters)
    index_row = lax.broadcasted_iota(jnp.int32, (filter_len, filter_len), 0)
    index_col = lax.broadcasted_iota(jnp.int32, (filter_len, filter_len), 1)
    lower_mask = (index_row >= index_col)[None]
    zero_half = jnp.zeros((), jnp.bfloat16)
    table_cur = jnp.where(lower_mask, circ_table, zero_half)
    table_prev = jnp.where(lower_mask, zero_half, circ_table)
    upstream_wide = upstream.astype(jnp.float32)
    mixed_rows = (upstream_wide * gate_values.astype(jnp.float32)).astype(jnp.bfloat16)
    tail_rows = passed_along(inputs, "zero", 1)
    head_rows = passed_along(mixed_rows, "zero", -1)
    input_ext = jnp.concatenate([tail_rows, inputs], axis=0)
    mixed_ext = jnp.concatenate([mixed_rows, head_rows], axis=0)
    input_blocks = blocked(input_ext, groups_all, filter_len)
    mixed_blocks = blocked(mixed_ext, groups_all, filter_len)
    input_cur = input_blocks[:, :, 1:]
    input_prev = input_blocks[:, :, :-1]
    mixed_own = mixed_blocks[:, :, :-1]
    mixed_next = mixed_blocks[:, :, 1:]
    conv_out = jnp.einsum(
        "gik,gcbk->gcbi", table_cur, input_cur, preferred_element_type=jnp.float32
    )
    conv_out = conv_out + jnp.einsum(
        "gik,gcbk->gcbi", table_prev, input_prev, preferred_element_type=jnp.float32
    )
    query_grad = (upstream_wide * unblocked(conv_out)).astype(jnp.bfloat16)
    back_blocks = jnp.einsum(
        "gki,gcbk->gcbi", table_cur, mixed_own, preferred_element_type=jnp.float32
    )
    back_blocks = back_blocks + jnp.einsum(
        "gki,gcbk->gcbi", table_prev, mixed_next, preferred_element_type=jnp.float32
    )
    input_grad = unblocked(back_blocks).astype(jnp.bfloat16)
    lag_cur = jnp.einsum("gcbi,gcbk->gik", mixed_own, input_cur, preferred_element_type=jnp.float32)
    lag_prev = jnp.einsum(
        "gcbi,gcbk->gik", mixed_own, input_prev, preferred_element_type=jnp.float32
    )
    square = filter_len * filter_len
    front_part = jnp.pad(
        jnp.where(lower_mask, lag_cur, 0.0).reshape(groups_all, square), ((0, 0), (filter_len, 0))
    )
    rear_part = jnp.pad(
        jnp.where(lower_mask, 0.0, lag_prev).reshape(groups_all, square), ((0, 0), (0, filter_len))
    )
    skewed = (front_part + rear_part).reshape(groups_all, filter_len, filter_len + 1).sum(axis=1)
    local_grad = skewed[:, 1:][:, ::-1]
    grad_full = lax.psum(local_grad.astype(jnp.bfloat16), "zero").astype(jnp.float32)
    total_sq = jnp.sum(grad_full * grad_full)
    grad_shard = lax.dynamic_slice_in_dim(
        grad_full, lax.axis_index("zero") * shard_len, shard_len, 0
    )
    clip_scale = jnp.minimum(1.0, CLIP_NORM / (jnp.sqrt(total_sq) + 1e-06))
    clipped = grad_shard * clip_scale
    step_count = step_index[0].astype(jnp.float32) + 1.0
    moment_one = BETA_ONE * first_moment[0] + (1.0 - BETA_ONE) * clipped
    moment_two = BETA_TWO * second_moment[0] + (1.0 - BETA_TWO) * clipped * clipped
    corrected_one = moment_one / (1.0 - jnp.power(BETA_ONE, step_count))
    corrected_two = moment_two / (1.0 - jnp.power(BETA_TWO, step_count))
    stepped = filters[0] - LEARN_RATE * corrected_one / (jnp.sqrt(corrected_two) + ADAM_EPS)
    bit_count = lax.axis_size("rep").bit_length() - 1
    partner_bit = step_index[0] % bit_count
    branches = [partial(swap_bit, bit_number=number) for number in range(bit_count)]
    partner_values = lax.switch(partner_bit, branches, stepped)
    new_filters = 0.5 * (stepped + partner_values)
    return (query_grad[None], input_grad[None], new_filters[None])


def solution(mesh):
    return jax.shard_map(
        on_device,
        mesh=mesh,
        in_specs=(
            P("rep", "zero", None),
            P("rep", "zero", None),
            P("rep", "zero", None),
            P("rep", "zero", None),
            P("rep", "zero", None),
            P("rep", "zero", None),
            P(),
        ),
        out_specs=(P("rep", "zero", None), P("rep", "zero", None), P("rep", "zero", None)),
        check_vma=False,
    )
```

profile of v0, /device:TPU:8, one launch (start us, length us, event | category | flops | bytes accessed | tf_op | source)
XLA Modules:
  0.0 408.8 jit_solution(13536019468429333070)
XLA Ops:
  9.8 23.5 %all_gather.3 = bf16[256,128]{1,0:T(8,128)(2,1)S(1)} all-gather(bf16[16,128]{1,0:T(8,128)(2,1)S(1)} %bitcast_convert_fusion), channel_id=1, replica_groups=mesh['rep'=2,'zero'=16] {'zero'}, dimensions={0}, use_global_device_ids=true | all-gather | bytes 69632 | tf_op jit(solution)/shard_map/all_gather | solution.py:58
  34.8 41.7 %copy.70 = bf16[32,8,128,256]{3,1,2,0:T(8,128)(2,1)S(1)} copy(bf16[32,8,128,256]{3,2,1,0:T(8,128)(2,1)S(1)} %bitcast.64) | data formatting | bytes 33554432
  76.5 6.6 %slice.29 = bf16[256,32640]{1,0:T(8,128)(2,1)} slice(bf16[256,32768]{1,0:T(8,128)(2,1)S(1)} %bitcast.65), slice={[0:256], [0:32640]} | slice | bytes 33423360 | tf_op jit(solution)/shard_map/slice | solution.py:31
  83.1 56.8 %reshape.85 = bf16[256,128,255]{2,1,0:T(8,128)(2,1)} reshape(bf16[256,32640]{1,0:T(8,128)(2,1)} %slice.29) | data formatting | bytes 33423360 | tf_op jit(solution)/shard_map/reshape | solution.py:32
  141.4 2.5 copy.52
  143.9 2.5 reshape.83
  146.4 3.0 fusion.25
  149.4 9.6 %fusion.1 = f32[256,16,128]{2,1,0:T(8,128)S(1)} fusion(pred[128,128]{1,0:T(8,128)(4,1)S(1)} %iota_compare_fusion, bf16[256,128,255]{2,1,0:T(8,128)(2,1)} %reshape.85, bf16[256,16,1,128]{3,2,1,0:T(2,128)(2,1)S(1)} %get-tuple-element.12), kind=kOutput, calls=%fused_computation.6 | convolution fusion | flops 138412032 | bytes 11550720 | tf_op jit(solution)/shard_map/gik,gcbk->gcbi/dot_general | solution.py:79
  159.1 11.7 %fusion.10 = f32[256,16,128]{2,1,0:T(8,128)} fusion(f32[256,16,128]{2,1,0:T(8,128)S(1)} %fusion.1, pred[128,128]{1,0:T(8,128)(4,1)S(1)} %iota_compare_fusion, bf16[256,128,255]{2,1,0:T(8,128)(2,1)} %reshape.85, bf16[256,16,1,128]{3,2,1,0:T(2,128)(2,1)S(1)} %get-tuple-element.11), kind=kOutput, calls=%fused_computation.20 | convolution fusion | flops 138936320 | bytes 13647872 | tf_op jit(solution)/shard_map/gik,gcbk->gcbi/dot_general | solution.py:82
  172.9 3.0 fusion.9
  175.9 3.7 collective-permute-start.1
  180.3 11.6 %collective-permute-done.1 = bf16[128,4096]{1,0:T(8,128)(2,1)} collective-permute-done((bf16[128,4096]{1,0:T(8,128)(2,1)S(1)}, bf16[128,4096]{1,0:T(8,128)(2,1)}, u32[]{:S(2)}, u32[]{:S(2)}) %collective-permute-start.1) | collective-permute-done | bytes 1048608 | tf_op jit(solution)/shard_map/ppermute | solution.py:23
  195.8 2.5 reshape.88
  198.3 3.8 fusion.24
  202.1 7.2 %convolution_select_fusion = f32[256,128,128]{2,1,0:T(8,128)} fusion(pred[128,128]{1,0:T(8,128)(4,1)S(1)} %iota_compare_fusion, bf16[256,16,1,128]{3,2,1,0:T(2,128)(2,1)S(1)} %copy-done.5, bf16[256,16,1,128]{3,2,1,0:T(2,128)(2,1)S(1)} %get-tuple-element.10), kind=kOutput, calls=%fused_computation.1 | convolution fusion | flops 138412032 | bytes 18890752 | tf_op jit(solution)/shard_map/gcbi,gcbk->gik/dot_general | solution.py:94
  209.3 7.1 %convolution_select_fusion.1 = f32[256,128,128]{2,1,0:T(8,128)} fusion(pred[128,128]{1,0:T(8,128)(4,1)S(1)} %iota_compare_fusion, bf16[256,16,1,128]{3,2,1,0:T(2,128)(2,1)S(1)} %copy-done.3, bf16[256,16,1,128]{3,2,1,0:T(2,128)(2,1)S(1)} %get-tuple-element.10), kind=kOutput, calls=%fused_computation.2 | convolution fusion | flops 138412032 | bytes 18890752 | tf_op jit(solution)/shard_map/gcbi,gcbk->gik/dot_general | solution.py:93
  216.4 17.7 %copy.64 = f32[256,128,128]{0,2,1:T(8,128)} copy(f32[256,128,128]{2,1,0:T(8,128)} %convolution_select_fusion) | data formatting | bytes 33554432 | tf_op jit(solution)/shard_map/reshape | solution.py:102
  234.1 17.7 %copy.63 = f32[256,128,128]{0,2,1:T(8,128)} copy(f32[256,128,128]{2,1,0:T(8,128)} %convolution_select_fusion.1) | data formatting | bytes 33554432 | tf_op jit(solution)/shard_map/reshape | solution.py:99
  251.9 18.0 %pad_add_fusion = f32[256,16512]{0,1:T(8,128)} fusion(f32[256,16384]{0,1:T(8,128)} %bitcast.62, f32[256,16384]{0,1:T(8,128)} %bitcast.63), kind=kLoop, calls=%fused_computation | loop fusion | flops 4227072 | bytes 50462720 | tf_op jit(solution)/shard_map/add | solution.py:104
  269.9 18.0 %reshape.93 = f32[256,128,129]{0,2,1:T(8,128)} reshape(f32[256,16512]{0,1:T(8,128)} %pad_add_fusion) | data formatting | bytes 33816576 | tf_op jit(solution)/shard_map/reshape | solution.py:104
  287.9 7.3 %reduce_sum.18 = bf16[256,129]{0,1:T(8,128)(2,1)S(1)} reduce(f32[256,128,129]{0,2,1:T(8,128)} %reshape.93, f32[]{:T(128)} %constant.9.clone.1), dimensions={1}, to_apply=%region_0.1 | reduce | flops 4194048 | bytes 16974340 | tf_op jit(solution)/shard_map/reduce_sum | solution.py:104
  296.2 10.4 %fusion = f32[256,16,128]{2,1,0:T(8,128)} fusion(pred[128,128]{1,0:T(8,128)(4,1)S(1)} %iota_compare_fusion, bf16[256,128,255]{2,1,0:T(8,128)(2,1)} %reshape.85, bf16[256,16,1,128]{3,2,1,0:T(2,128)(2,1)S(1)} %copy-done.1), kind=kOutput, calls=%fused_computation.5 | convolution fusion | flops 138412032 | bytes 11550720 | tf_op jit(solution)/shard_map/gki,gcbk->gcbi/dot_general | solution.py:86
  306.5 78.4 %all-reduce.4.cloned.1.call-done = bf16[256,128]{1,0:T(8,128)(2,1)} async-done(((bf16[256,128]{1,0:T(8,128)(2,1)}), bf16[256,128]{1,0:T(8,128)(2,1)}) %all-reduce.4.cloned.1.call-update) | async-done | bytes 65552 | tf_op jit(solution)/shard_map/psum | solution.py:106
  389.6 10.4 %add_convert_fusion = bf16[256,16,128]{2,1,0:T(8,128)(2,1)S(1)} fusion(f32[256,16,128]{2,1,0:T(8,128)} %fusion, pred[128,128]{1,0:T(8,128)(4,1)S(1)} %iota_compare_fusion, bf16[256,128,255]{2,1,0:T(8,128)(2,1)} %reshape.85, bf16[256,16,1,128]{3,2,1,0:T(2,128)(2,1)} %get-tuple-element.9), kind=kOutput, calls=%fused_computation.19 | convolution fusion | flops 139460608 | bytes 13647872 | tf_op jit(solution)/shard_map/gki,gcbk->gcbi/dot_general | solution.py:89
  (43 shorter events, 18.3 us)
Async XLA Ops:
  7.2 377.8 %all-reduce.4.cloned.1.call-start = ((), (), s32[]{:S(2)}) async-start(), calls=%async_computation | async-start | bytes 131072 | tf_op jit(solution)/shard_map/psum | solution.py:106
  7.2 132.8 %collective-permute-start = (bf16[128,4096]{1,0:T(8,128)(2,1)}, bf16[128,4096]{1,0:T(8,128)(2,1)}, u32[]{:S(2)}, u32[]{:S(2)}) collective-permute-start(bf16[128,4096]{1,0:T(8,128)(2,1)} %bitcast.69), channel_id=1, source_target_pairs={{0,1},{1,2},{2,3},{3,4},{4,5},{5,6},{6,7},{7,8},{8,9},{9,10},{10,1... | collective-permute-start | bytes 3145736 | tf_op jit(solution)/shard_map/ppermute | solution.py:23
  83.1 56.8 %copy-start.6 = (bf16[1,128,4096]{2,1,0:T(8,128)(2,1)S(1)}, bf16[1,128,4096]{2,1,0:T(8,128)(2,1)}, u32[]{:S(2)}) copy-start(bf16[1,128,4096]{2,1,0:T(8,128)(2,1)} %param.7) | copy-start | bytes 3145732
  149.4 9.7 %copy-start.2 = (bf16[256,16,1,128]{3,2,1,0:T(2,128)(2,1)}, bf16[256,16,1,128]{3,2,1,0:T(2,128)(2,1)S(1)}, u32[]{:S(2)}) copy-start(bf16[256,16,1,128]{3,2,1,0:T(2,128)(2,1)S(1)} %get-tuple-element.12) | copy-start | bytes 3145732
  149.4 9.7 %copy-start.4 = (bf16[256,16,1,128]{3,2,1,0:T(2,128)(2,1)}, bf16[256,16,1,128]{3,2,1,0:T(2,128)(2,1)S(1)}, u32[]{:S(2)}) copy-start(bf16[256,16,1,128]{3,2,1,0:T(2,128)(2,1)S(1)} %get-tuple-element.11) | copy-start | bytes 3145732
  175.9 16.0 %collective-permute-start.1 = (bf16[128,4096]{1,0:T(8,128)(2,1)S(1)}, bf16[128,4096]{1,0:T(8,128)(2,1)}, u32[]{:S(2)}, u32[]{:S(2)}) collective-permute-start(bf16[128,4096]{1,0:T(8,128)(2,1)S(1)} %get-tuple-element.13), channel_id=1, source_target_pairs={{1,0},{2,1},{3,2},{4,3},{5,4},{6,5},{7,6},{8,7},{9,8},{10,9},{11,1... | collective-permute-start | bytes 3145736 | tf_op jit(solution)/shard_map/ppermute | solution.py:23
  198.3 3.8 copy-start.5
  202.1 7.2 %copy-start = (bf16[256,16,1,128]{3,2,1,0:T(2,128)(2,1)}, bf16[256,16,1,128]{3,2,1,0:T(2,128)(2,1)S(1)}, u32[]{:S(2)}) copy-start(bf16[256,16,1,128]{3,2,1,0:T(2,128)(2,1)S(1)} %get-tuple-element.10) | copy-start | bytes 3145732
  202.1 7.2 %copy-start.3 = (bf16[256,16,1,128]{3,2,1,0:T(2,128)(2,1)S(1)}, bf16[256,16,1,128]{3,2,1,0:T(2,128)(2,1)}, u32[]{:S(2)}) copy-start(bf16[256,16,1,128]{3,2,1,0:T(2,128)(2,1)} %copy-done.2) | copy-start | bytes 3145732
  287.9 8.3 %copy-start.1 = (bf16[256,16,1,128]{3,2,1,0:T(2,128)(2,1)S(1)}, bf16[256,16,1,128]{3,2,1,0:T(2,128)(2,1)}, u32[]{:S(2)}) copy-start(bf16[256,16,1,128]{3,2,1,0:T(2,128)(2,1)} %copy-done) | copy-start | bytes 3145732
  296.1 91.9 %copy-start.7 = (f32[1,16,128]{2,1,0:T(8,128)S(1)}, f32[1,16,128]{2,1,0:T(8,128)}, u32[]{:S(2)}) copy-start(f32[1,16,128]{2,1,0:T(8,128)} %param.10) | copy-start | bytes 24580
  296.2 91.9 %copy-start.8 = (f32[1,16,128]{2,1,0:T(8,128)S(1)}, f32[1,16,128]{2,1,0:T(8,128)}, u32[]{:S(2)}) copy-start(f32[1,16,128]{2,1,0:T(8,128)} %param.12) | copy-start | bytes 24580
  296.2 91.9 %copy-start.9 = (f32[1,16,128]{2,1,0:T(8,128)S(1)}, f32[1,16,128]{2,1,0:T(8,128)}, u32[]{:S(2)}) copy-start(f32[1,16,128]{2,1,0:T(8,128)} %param.11) | copy-start | bytes 24580
  388.1 13.2 %collective-permute-start.2 = (f32[16,128]{1,0:T(8,128)S(1)}, f32[16,128]{1,0:T(8,128)S(1)}, u32[]{:S(2)}, u32[]{:S(2)}) collective-permute-start(f32[16,128]{1,0:T(8,128)S(1)} %fusion.17), channel_id=1, source_target_pairs={{0,16},{16,0},{1,17},{17,1},{2,18},{18,2},{3,19},{19,3},{4,20},{20... | collective-permute-start | bytes 24584 | tf_op jit(solution)/shard_map/ppermute | solution.py:17
Sparse Core Ops, SparseCore 0:
  296.3 88.6 all-reduce.3
where the time goes:
time: 410 us; the launch traced here: 409 us
  local copies, waits for them, and re-layouts  181 us (44%)
  waiting for transfers between devices  90 us (22%)
  matrix products  56.3 us (14%)
  other arithmetic  34.8 us (8%)
  blocking collectives  23.5 us (6%)
  between operations  15.7 us (4%)
  starting transfers between devices  7.19 us (2%)
    psum x1, waiting for transfers between devices, on_device(): lax.psum(local_grad.astype(jnp.bfloat16), 'zero').astype(jnp.float32)  78.4 us
    reshape x1, local copies, waits for them, and re-layouts, circulant(): trimmed.reshape(groups_all, filter_len, 2 * filter_len - 1)  56.8 us
    unnamed x22, local copies, waits for them, and re-layouts  41.9 us
    all_gather x1, blocking collectives, on_device(): lax.all_gather(filters[0].astype(jnp.bfloat16), 'zero', axis=0, tiled=True)  23.5 us
    add x1, other arithmetic, on_device(): front_part + rear_part  18 us
    reshape x1, local copies, waits for them, and re-layouts, on_device(): (front_part + rear_part).reshape(groups_all, filter_len, filter_len + 1)  18 us
    reshape x1, local copies, waits for them, and re-layouts, on_device(): jnp.where(lower_mask, 0.0, lag_prev).reshape(groups_all, square)  17.7 us
    reshape x1, local copies, waits for them, and re-layouts, on_device(): jnp.where(lower_mask, lag_cur, 0.0).reshape(groups_all, square)  17.7 us
  transfers between devices with their start and end apart: 4, of which 2 were waited for; matrix products, arithmetic and copies ran while one was open for 32% of the time, Pallas kernels for 0%

commit v1 on v0

--- a/solution.py
+++ b/solution.py
@@ -103,7 +103,9 @@
     )
     skewed = (front_part + rear_part).reshape(groups_all, filter_len, filter_len + 1).sum(axis=1)
     local_grad = skewed[:, 1:][:, ::-1]
-    grad_full = lax.psum(local_grad.astype(jnp.bfloat16), "zero").astype(jnp.float32)
+    grad_full = jnp.sum(lax.all_gather(local_grad.astype(jnp.bfloat16), "zero"), axis=0).astype(
+        jnp.float32
+    )
     total_sq = jnp.sum(grad_full * grad_full)
     grad_shard = lax.dynamic_slice_in_dim(
         grad_full, lax.axis_index("zero") * shard_len, shard_len, 0

time: 410 us -> 358 us (0.87)
  waiting for transfers between devices: 90 us -> 37.8 us
    psum x1 -> x0, waiting for transfers between devices: 78.4 us -> none  [on_device(): lax.psum(local_grad.astype(jnp.bfloat16), 'zero').astype(jnp.float32)]
    all_gather x0 -> x1, waiting for transfers between devices: none -> 25.5 us  [on_device(): lax.all_gather(local_grad.astype(jnp.bfloat16), 'zero')]
    unnamed x22 -> x24, local copies, waits for them, and re-layouts: 41.9 us -> 43.2 us
  transfers between devices with their start and end apart: 4 -> 4, of which waited for: 2 -> 2; matrix products, arithmetic and copies ran while one was open for 32% -> 36% of each run, Pallas kernels for 0% -> 0%
where the time goes in v1:
time: 358 us; the launch traced here: 355 us
  local copies, waits for them, and re-layouts  183 us (51%)
  matrix products  56.3 us (16%)
  waiting for transfers between devices  37.8 us (11%)
  other arithmetic  32 us (9%)
  blocking collectives  23.5 us (7%)
  between operations  15.8 us (4%)
  starting transfers between devices  7.18 us (2%)
    reshape x1, local copies, waits for them, and re-layouts, circulant(): trimmed.reshape(groups_all, filter_len, 2 * filter_len - 1)  56.8 us
    unnamed x24, local copies, waits for them, and re-layouts  43.2 us
    all_gather x1, waiting for transfers between devices, on_device(): lax.all_gather(local_grad.astype(jnp.bfloat16), 'zero')  25.5 us
    all_gather x1, blocking collectives, on_device(): lax.all_gather(filters[0].astype(jnp.bfloat16), 'zero', axis=0, tiled=True)  23.5 us
    add x1, other arithmetic, on_device(): front_part + rear_part  18 us
    reshape x1, local copies, waits for them, and re-layouts, on_device(): (front_part + rear_part).reshape(groups_all, filter_len, filter_len + 1)  18 us
    reshape x1, local copies, waits for them, and re-layouts, on_device(): jnp.where(lower_mask, 0.0, lag_prev).reshape(groups_all, square)  17.7 us
    reshape x1, local copies, waits for them, and re-layouts, on_device(): jnp.where(lower_mask, lag_cur, 0.0).reshape(groups_all, square)  17.7 us
  transfers between devices with their start and end apart: 4, of which 2 were waited for; matrix products, arithmetic and copies ran while one was open for 36% of the time, Pallas kernels for 0%

profile of v1, /device:TPU:8, one launch (start us, length us, event | category | flops | bytes accessed | tf_op | source)
XLA Modules:
  0.0 355.2 jit_solution(11276275509142895479)
XLA Ops:
  9.8 23.5 %all_gather.9 = bf16[256,128]{1,0:T(8,128)(2,1)S(1)} all-gather(bf16[16,128]{1,0:T(8,128)(2,1)S(1)} %bitcast_convert_fusion), channel_id=1, replica_groups=mesh['rep'=2,'zero'=16] {'zero'}, dimensions={0}, use_global_device_ids=true | all-gather | bytes 69632 | tf_op jit(solution)/shard_map/all_gather | solution.py:58
  34.8 41.7 %copy.79 = bf16[32,8,128,256]{3,1,2,0:T(8,128)(2,1)S(1)} copy(bf16[32,8,128,256]{3,2,1,0:T(8,128)(2,1)S(1)} %bitcast.69) | data formatting | bytes 33554432
  76.5 6.6 %slice.29 = bf16[256,32640]{1,0:T(8,128)(2,1)} slice(bf16[256,32768]{1,0:T(8,128)(2,1)S(1)} %bitcast.70), slice={[0:256], [0:32640]} | slice | bytes 33423360 | tf_op jit(solution)/shard_map/slice | solution.py:31
  83.2 56.8 %reshape.85 = bf16[256,128,255]{2,1,0:T(8,128)(2,1)} reshape(bf16[256,32640]{1,0:T(8,128)(2,1)} %slice.29) | data formatting | bytes 33423360 | tf_op jit(solution)/shard_map/reshape | solution.py:32
  143.9 2.5 reshape.83
  146.4 3.0 fusion.25
  149.4 9.6 %fusion.1 = f32[256,16,128]{2,1,0:T(8,128)S(1)} fusion(pred[128,128]{1,0:T(8,128)(4,1)S(1)} %iota_compare_fusion, bf16[256,128,255]{2,1,0:T(8,128)(2,1)} %reshape.85, bf16[256,16,1,128]{3,2,1,0:T(2,128)(2,1)S(1)} %get-tuple-element.12), kind=kOutput, calls=%fused_computation.6 | convolution fusion | flops 138412032 | bytes 11550720 | tf_op jit(solution)/shard_map/gik,gcbk->gcbi/dot_general | solution.py:79
  159.1 11.7 %fusion.10 = f32[256,16,128]{2,1,0:T(8,128)} fusion(f32[256,16,128]{2,1,0:T(8,128)S(1)} %fusion.1, pred[128,128]{1,0:T(8,128)(4,1)S(1)} %iota_compare_fusion, bf16[256,128,255]{2,1,0:T(8,128)(2,1)} %reshape.85, bf16[256,16,1,128]{3,2,1,0:T(2,128)(2,1)S(1)} %get-tuple-element.11), kind=kOutput, calls=%fused_computation.20 | convolution fusion | flops 138936320 | bytes 13647872 | tf_op jit(solution)/shard_map/gik,gcbk->gcbi/dot_general | solution.py:82
  173.0 2.6 fusion.9
  175.6 3.7 %collective-permute-start.1 = (bf16[128,4096]{1,0:T(8,128)(2,1)S(1)}, bf16[128,4096]{1,0:T(8,128)(2,1)S(1)}, u32[]{:S(2)}, u32[]{:S(2)}) collective-permute-start(bf16[128,4096]{1,0:T(8,128)(2,1)S(1)} %get-tuple-element.13), channel_id=1, source_target_pairs={{1,0},{2,1},{3,2},{4,3},{5,4},{6,5},{7,6},{8,7},{9,8},{10,9},{11,1... | collective-permute-start | bytes 3145736 | tf_op jit(solution)/shard_map/ppermute | solution.py:23
  179.3 12.3 %collective-permute-done.1 = bf16[128,4096]{1,0:T(8,128)(2,1)S(1)} collective-permute-done((bf16[128,4096]{1,0:T(8,128)(2,1)S(1)}, bf16[128,4096]{1,0:T(8,128)(2,1)S(1)}, u32[]{:S(2)}, u32[]{:S(2)}) %collective-permute-start.1) | collective-permute-done | bytes 1048608 | tf_op jit(solution)/shard_map/ppermute | solution.py:23
  191.7 2.5 copy.66
  194.2 2.5 reshape.88
  196.8 3.8 %fusion.24 = (bf16[256,16,1,128]{3,2,1,0:T(2,128)(2,1)}, bf16[256,16,1,128]{3,2,1,0:T(2,128)(2,1)S(1)}) fusion(bf16[256,16,2,128]{3,2,1,0:T(2,128)(2,1)S(1)} %reshape.88), kind=kLoop, calls=%fused_computation.46 | loop fusion | bytes 4194304 | tf_op jit(solution)/shard_map/slice | solution.py:78
  200.6 7.2 %convolution_select_fusion = f32[256,128,128]{2,1,0:T(8,128)} fusion(pred[128,128]{1,0:T(8,128)(4,1)S(1)} %iota_compare_fusion, bf16[256,16,1,128]{3,2,1,0:T(2,128)(2,1)S(1)} %copy-done.5, bf16[256,16,1,128]{3,2,1,0:T(2,128)(2,1)S(1)} %get-tuple-element.10), kind=kOutput, calls=%fused_computation.1 | convolution fusion | flops 138412032 | bytes 18890752 | tf_op jit(solution)/shard_map/gcbi,gcbk->gik/dot_general | solution.py:94
  207.7 7.1 %convolution_select_fusion.1 = f32[256,128,128]{2,1,0:T(8,128)} fusion(pred[128,128]{1,0:T(8,128)(4,1)S(1)} %iota_compare_fusion, bf16[256,16,1,128]{3,2,1,0:T(2,128)(2,1)S(1)} %copy-done.3, bf16[256,16,1,128]{3,2,1,0:T(2,128)(2,1)S(1)} %get-tuple-element.10), kind=kOutput, calls=%fused_computation.2 | convolution fusion | flops 138412032 | bytes 18890752 | tf_op jit(solution)/shard_map/gcbi,gcbk->gik/dot_general | solution.py:93
  214.8 17.7 %copy.74 = f32[256,128,128]{0,2,1:T(8,128)} copy(f32[256,128,128]{2,1,0:T(8,128)} %convolution_select_fusion) | data formatting | bytes 33554432 | tf_op jit(solution)/shard_map/reshape | solution.py:102
  232.6 17.7 %copy.73 = f32[256,128,128]{0,2,1:T(8,128)} copy(f32[256,128,128]{2,1,0:T(8,128)} %convolution_select_fusion.1) | data formatting | bytes 33554432 | tf_op jit(solution)/shard_map/reshape | solution.py:99
  250.3 18.0 %pad_add_fusion = f32[256,16512]{0,1:T(8,128)} fusion(f32[256,16384]{0,1:T(8,128)} %bitcast.67, f32[256,16384]{0,1:T(8,128)} %bitcast.68), kind=kLoop, calls=%fused_computation | loop fusion | flops 4227072 | bytes 50462720 | tf_op jit(solution)/shard_map/add | solution.py:104
  268.3 18.0 %reshape.93 = f32[256,128,129]{0,2,1:T(8,128)} reshape(f32[256,16512]{0,1:T(8,128)} %pad_add_fusion) | data formatting | bytes 33816576 | tf_op jit(solution)/shard_map/reshape | solution.py:104
  286.3 7.3 %reduce_sum.30 = bf16[256,129]{0,1:T(8,128)(2,1)S(1)} reduce(f32[256,128,129]{0,2,1:T(8,128)} %reshape.93, f32[]{:T(128)} %constant.10.clone.1), dimensions={1}, to_apply=%region_0.1 | reduce | flops 4194048 | bytes 16974340 | tf_op jit(solution)/shard_map/reduce_sum | solution.py:104
  295.1 10.4 %fusion = f32[256,16,128]{2,1,0:T(8,128)} fusion(pred[128,128]{1,0:T(8,128)(4,1)S(1)} %iota_compare_fusion, bf16[256,128,255]{2,1,0:T(8,128)(2,1)} %reshape.85, bf16[256,16,1,128]{3,2,1,0:T(2,128)(2,1)S(1)} %copy-done.1), kind=kOutput, calls=%fused_computation.5 | convolution fusion | flops 138412032 | bytes 11550720 | tf_op jit(solution)/shard_map/gki,gcbk->gcbi/dot_general | solution.py:86
  305.5 25.5 %all-gather.3.cloned.1.call-done = bf16[4096,128]{0,1:T(8,128)(2,1)} async-done(((bf16[256,128]{0,1:T(8,128)(2,1)}), bf16[4096,128]{0,1:T(8,128)(2,1)}) %all-gather.3.cloned.1.call-update) | async-done | bytes 1048592 | tf_op jit(solution)/shard_map/all_gather | solution.py:106
  336.1 10.4 %add_convert_fusion = bf16[256,16,128]{2,1,0:T(8,128)(2,1)S(1)} fusion(f32[256,16,128]{2,1,0:T(8,128)} %fusion, pred[128,128]{1,0:T(8,128)(4,1)S(1)} %iota_compare_fusion, bf16[256,128,255]{2,1,0:T(8,128)(2,1)} %reshape.85, bf16[256,16,1,128]{3,2,1,0:T(2,128)(2,1)} %get-tuple-element.9), kind=kOutput, calls=%fused_computation.19 | convolution fusion | flops 139460608 | bytes 13647872 | tf_op jit(solution)/shard_map/gki,gcbk->gcbi/dot_general | solution.py:89
  (47 shorter events, 17.4 us)
Async XLA Ops:
  7.2 323.8 %all-gather.3.cloned.1.call-start = ((), (), s32[]{:S(2)}) async-start(), calls=%async_computation | async-start | bytes 1114112 | tf_op jit(solution)/shard_map/all_gather | solution.py:106
  7.2 132.8 %collective-permute-start = (bf16[128,4096]{1,0:T(8,128)(2,1)}, bf16[128,4096]{1,0:T(8,128)(2,1)}, u32[]{:S(2)}, u32[]{:S(2)}) collective-permute-start(bf16[128,4096]{1,0:T(8,128)(2,1)} %bitcast.75), channel_id=1, source_target_pairs={{0,1},{1,2},{2,3},{3,4},{4,5},{5,6},{6,7},{7,8},{8,9},{9,10},{10,1... | collective-permute-start | bytes 3145736 | tf_op jit(solution)/shard_map/ppermute | solution.py:23
  83.1 56.8 %copy-start.6 = (bf16[1,128,4096]{2,1,0:T(8,128)(2,1)S(1)}, bf16[1,128,4096]{2,1,0:T(8,128)(2,1)}, u32[]{:S(2)}) copy-start(bf16[1,128,4096]{2,1,0:T(8,128)(2,1)} %param.7) | copy-start | bytes 3145732
  149.4 9.7 %copy-start.2 = (bf16[256,16,1,128]{3,2,1,0:T(2,128)(2,1)}, bf16[256,16,1,128]{3,2,1,0:T(2,128)(2,1)S(1)}, u32[]{:S(2)}) copy-start(bf16[256,16,1,128]{3,2,1,0:T(2,128)(2,1)S(1)} %get-tuple-element.12) | copy-start | bytes 3145732
  149.4 9.7 %copy-start.4 = (bf16[256,16,1,128]{3,2,1,0:T(2,128)(2,1)}, bf16[256,16,1,128]{3,2,1,0:T(2,128)(2,1)S(1)}, u32[]{:S(2)}) copy-start(bf16[256,16,1,128]{3,2,1,0:T(2,128)(2,1)S(1)} %get-tuple-element.11) | copy-start | bytes 3145732
  170.7 2.2 copy-start.7
  175.6 16.0 %collective-permute-start.1 = (bf16[128,4096]{1,0:T(8,128)(2,1)S(1)}, bf16[128,4096]{1,0:T(8,128)(2,1)S(1)}, u32[]{:S(2)}, u32[]{:S(2)}) collective-permute-start(bf16[128,4096]{1,0:T(8,128)(2,1)S(1)} %get-tuple-element.13), channel_id=1, source_target_pairs={{1,0},{2,1},{3,2},{4,3},{5,4},{6,5},{7,6},{8,7},{9,8},{10,9},{11,1... | collective-permute-start | bytes 3145736 | tf_op jit(solution)/shard_map/ppermute | solution.py:23
  196.7 3.8 %copy-start.5 = (bf16[256,16,1,128]{3,2,1,0:T(2,128)(2,1)S(1)}, bf16[256,16,1,128]{3,2,1,0:T(2,128)(2,1)}, u32[]{:S(2)}) copy-start(bf16[256,16,1,128]{3,2,1,0:T(2,128)(2,1)} %copy-done.4) | copy-start | bytes 3145732
  200.6 7.2 %copy-start = (bf16[256,16,1,128]{3,2,1,0:T(2,128)(2,1)}, bf16[256,16,1,128]{3,2,1,0:T(2,128)(2,1)S(1)}, u32[]{:S(2)}) copy-start(bf16[256,16,1,128]{3,2,1,0:T(2,128)(2,1)S(1)} %get-tuple-element.10) | copy-start | bytes 3145732
  200.6 7.2 %copy-start.3 = (bf16[256,16,1,128]{3,2,1,0:T(2,128)(2,1)S(1)}, bf16[256,16,1,128]{3,2,1,0:T(2,128)(2,1)}, u32[]{:S(2)}) copy-start(bf16[256,16,1,128]{3,2,1,0:T(2,128)(2,1)} %copy-done.2) | copy-start | bytes 3145732
  286.3 8.8 %copy-start.1 = (bf16[256,16,1,128]{3,2,1,0:T(2,128)(2,1)S(1)}, bf16[256,16,1,128]{3,2,1,0:T(2,128)(2,1)}, u32[]{:S(2)}) copy-start(bf16[256,16,1,128]{3,2,1,0:T(2,128)(2,1)} %copy-done) | copy-start | bytes 3145732
  295.1 39.4 %copy-start.8 = (f32[1,16,128]{2,1,0:T(8,128)S(1)}, f32[1,16,128]{2,1,0:T(8,128)}, u32[]{:S(2)}) copy-start(f32[1,16,128]{2,1,0:T(8,128)} %param.10) | copy-start | bytes 24580
  295.1 39.4 %copy-start.9 = (f32[1,16,128]{2,1,0:T(8,128)S(1)}, f32[1,16,128]{2,1,0:T(8,128)}, u32[]{:S(2)}) copy-start(f32[1,16,128]{2,1,0:T(8,128)} %param.12) | copy-start | bytes 24580
  295.1 39.4 %copy-start.10 = (f32[1,16,128]{2,1,0:T(8,128)S(1)}, f32[1,16,128]{2,1,0:T(8,128)}, u32[]{:S(2)}) copy-start(f32[1,16,128]{2,1,0:T(8,128)} %param.11) | copy-start | bytes 24580
  334.6 13.2 %collective-permute-start.2 = (f32[16,128]{1,0:T(8,128)S(1)}, f32[16,128]{1,0:T(8,128)S(1)}, u32[]{:S(2)}, u32[]{:S(2)}) collective-permute-start(f32[16,128]{1,0:T(8,128)S(1)} %fusion.17), channel_id=1, source_target_pairs={{0,16},{16,0},{1,17},{17,1},{2,18},{18,2},{3,19},{19,3},{4,20},{20... | collective-permute-start | bytes 24584 | tf_op jit(solution)/shard_map/ppermute | solution.py:17
Sparse Core Ops, SparseCore 0:
  294.5 36.4 all-gather.2
